TPU v7x, 32 devices: a whole 2x2x4 slice. The times are simulated.
32 devices in a mesh: section: 2 (over core), expert: 16 (over z, y, x).
Axes of the slice: x: 2, y: 2, z: 4, core: 2. Of those that a mesh axis runs over, the one named last changes fastest.
Arguments:
- block_input: bfloat16 [2, 8192, 768], P(None, 'expert'), may hold values from -6 to 6
- cotangent: bfloat16 [2, 8192, 768], P(None, 'expert'), may hold values from -6 to 6
- expert_ids: int32 [2, 2, 8192, 2], P(None, None, 'expert'), may hold values from 0 to 15, all different within a row; in each aligned block of 512 rows (0 to 511, 512 to 1023, ..., all dimensions but the last counted through in order) at most 68 rows name the same one
- qkv_weight: bfloat16 [2, 768, 2304], P('section'), may hold values from -0.21875 to 0.21875
- query_bias: float32 [2, 768], P('section'), may hold values from -4 to 4
- value_bias: float32 [2, 768], P('section'), may hold values from -1.5 to 1.5
- proj_weight: bfloat16 [2, 768, 768], P('section'), may hold values from -1.75 to 1.75
- proj_bias: float32 [2, 768], P('section'), may hold values from -4 to 4
- attn_gain: float32 [2, 768], P('section'), may hold values from 0.25 to 1.75
- ffn_gain: float32 [2, 768], P('section'), may hold values from 0.25 to 1.75
- router_weight: bfloat16 [2, 768, 16], P('section'), may hold values from -0.4375 to 0.4375
- in_weight: bfloat16 [2, 16, 768, 3072], P('section', 'expert'), may hold values from -0.21875 to 0.21875
- out_weight: bfloat16 [2, 16, 3072, 768], P('section', 'expert'), may hold values from -0.109375 to 0.109375
Outputs:
- section_out: bfloat16 [2, 2, 8192, 768], P('section', None, 'expert')
- section_grad: float32 [2, 2, 8192, 768], P('section', None, 'expert')
- grad_qkv: float32 [2, 768, 2304], P('section')
- grad_qbias: float32 [2, 768], P('section')
- grad_vbias: float32 [2, 768], P('section')
- grad_proj: float32 [2, 768, 768], P('section')
- grad_pbias: float32 [2, 768], P('section')
- grad_attngain: float32 [2, 768], P('section')
- grad_ffngain: float32 [2, 768], P('section')
- grad_router: float32 [2, 768, 16], P('section')
- grad_win: bfloat16 [2, 16, 768, 3072], P('section', 'expert')
- grad_wout: bfloat16 [2, 16, 3072, 768], P('section', 'expert')
Inputs may be any that keep to these rules, and one draw needn't show every extreme that they name: `expert_ids`: A token's 2 ids differ. For each layer and micro-batch, among the choices of the 512 tokens of one device, no expert is named more than 68 times, a bound that some block reaches.
All inputs are finite; a program needn't handle non-finite values.
Results may differ from a plain program's by a relative error of at most 0.02.
Values may be sent and summed in bfloat16 or wider, within the bound.
A program may use at most 384 MiB of HBM per device.

v0:
```python
import jax
import jax.numpy as jnp
from jax import lax
from jax.sharding import PartitionSpec as P

HD = 64
SEQ = 512


EPS = 1e-06
NEG = -1e30


def shifted(array, axis, by):
    size = lax.axis_size(axis)
    pairs = [(i, i + by) for i in range(size) if 0 <= i + by < size]
    return lax.ppermute(array, axis, pairs)


def norm_apply(field, scaling):
    return field * lax.rsqrt(jnp.mean(field * field, axis=-1, keepdims=True) + EPS) * scaling


def router_gates(logits, choose):
    probs_all = jax.nn.softmax(logits, axis=-1)
    picked = jnp.sum(probs_all[:, None, :] * choose, axis=-1)
    return picked / jnp.sum(picked, axis=-1, keepdims=True)


def capacity_of(tokens, choices, experts):
    return tokens * choices // experts + max(1, tokens * choices // (16 * experts))


def one_hot_ids(route_ids, experts):
    return (route_ids[:, :, None] == jnp.arange(experts, dtype=jnp.int32)[None, None, :]).astype(
        jnp.float32
    )


def slot_plan(route_ids, experts, capacity):
    flat_ids = route_ids.reshape(-1)
    marked = (flat_ids[:, None] == jnp.arange(experts, dtype=jnp.int32)[None, :]).astype(jnp.int32)
    ranked = jnp.sum(jnp.cumsum(marked, axis=0) * marked, axis=-1) - 1
    slot_ids = flat_ids * capacity + ranked
    source = (
        jnp.zeros((experts * capacity,), jnp.int32)
        .at[slot_ids]
        .set(jnp.arange(flat_ids.shape[0], dtype=jnp.int32))
    )
    filled = jnp.zeros((experts * capacity,), jnp.int32).at[slot_ids].set(1)
    return (slot_ids, source, filled)


def pack_rows(row_data, source, filled, experts, capacity):
    taken = jnp.take(row_data, source, axis=0)
    blank = jnp.zeros((), row_data.dtype)
    return jnp.where(filled[:, None] > 0, taken, blank).reshape(
        experts, capacity, row_data.shape[1]
    )


def causal_scores(queries, key_rows):
    scores = jnp.einsum(
        "qhd,khd->hqk", queries, key_rows, preferred_element_type=jnp.float32
    ) * HD ** (-0.5)
    length = scores.shape[-1]
    causal = jnp.arange(length)[:, None] >= jnp.arange(length)[None, :]
    return jnp.where(causal[None], scores, NEG)


def attend_forward(block_set):
    queries, key_rows, value_rows = block_set
    scores = causal_scores(queries, key_rows)
    row_max = jnp.max(scores, axis=-1, keepdims=True)
    weights = jnp.exp(scores - row_max)
    row_total = jnp.sum(weights, axis=-1, keepdims=True)
    prob_low = (weights / row_total).astype(jnp.bfloat16)
    attended = jnp.einsum("hqk,khd->qhd", prob_low, value_rows, preferred_element_type=jnp.float32)
    return (attended.astype(jnp.bfloat16), row_max[..., 0] + jnp.log(row_total[..., 0]))


def attend_backward(block_set):
    queries, key_rows, value_rows, log_total, grad_out = block_set
    scores = causal_scores(queries, key_rows)
    weights = jnp.exp(scores - log_total[..., None])
    grad_probs = jnp.einsum(
        "qhd,khd->hqk", grad_out, value_rows, preferred_element_type=jnp.float32
    )
    inner = jnp.sum(weights * grad_probs, axis=-1, keepdims=True)
    grad_scores = (weights * (grad_probs - inner)).astype(jnp.bfloat16)
    grad_value = jnp.einsum(
        "hqk,qhd->khd", weights.astype(jnp.bfloat16), grad_out, preferred_element_type=jnp.float32
    )
    grad_query = jnp.einsum(
        "hqk,khd->qhd", grad_scores, key_rows, preferred_element_type=jnp.float32
    ) * HD ** (-0.5)
    grad_key = jnp.einsum(
        "hqk,qhd->khd", grad_scores, queries, preferred_element_type=jnp.float32
    ) * HD ** (-0.5)
    return (grad_query, grad_key, grad_value)


def layer_forward(current, route_ids, weights):
    (
        qkv_weight,
        query_bias,
        value_bias,
        proj_weight,
        proj_bias,
        attn_gain,
        ffn_gain,
        router_weight,
        in_weight,
        out_weight,
    ) = weights
    tokens, model_width = current.shape
    choices = route_ids.shape[1]
    experts = router_weight.shape[1]
    capacity = capacity_of(tokens, choices, experts)
    normed = norm_apply(current, attn_gain).astype(jnp.bfloat16)
    packed = jnp.dot(normed, qkv_weight, preferred_element_type=jnp.float32)
    queries = (packed[:, :model_width] + query_bias).astype(jnp.bfloat16)
    key_rows = packed[:, model_width : 2 * model_width].astype(jnp.bfloat16)
    value_rows = (packed[:, 2 * model_width :] + value_bias).astype(jnp.bfloat16)
    grid_shape = (tokens // SEQ, SEQ, model_width // HD, HD)
    attended, log_total = lax.map(
        attend_forward,
        (queries.reshape(grid_shape), key_rows.reshape(grid_shape), value_rows.reshape(grid_shape)),
    )
    attended = attended.reshape(tokens, model_width)
    between_sections = current + (
        jnp.dot(attended, proj_weight, preferred_element_type=jnp.float32) + proj_bias
    )
    routed = norm_apply(between_sections, ffn_gain).astype(jnp.bfloat16)
    logits = jnp.dot(routed, router_weight, preferred_element_type=jnp.float32)
    gating = router_gates(logits, one_hot_ids(route_ids, experts))
    slot_ids, source, filled = slot_plan(route_ids, experts, capacity)
    sending = pack_rows(routed, source // choices, filled, experts, capacity)
    arrived = lax.all_to_all(sending, "expert", split_axis=0, concat_axis=0, tiled=True)
    groups = lax.axis_size("expert")
    local_count = in_weight.shape[0]
    slot_count = arrived.shape[1]
    row_data = arrived.reshape(groups, local_count, slot_count, model_width)
    hidden = jnp.einsum("necd,edf->necf", row_data, in_weight, preferred_element_type=jnp.float32)
    active = jax.nn.gelu(hidden).astype(jnp.bfloat16)
    produced = jnp.einsum("necf,efd->necd", active, out_weight, preferred_element_type=jnp.float32)
    produced = produced.astype(jnp.bfloat16).reshape(groups * local_count, slot_count, model_width)
    returned = lax.all_to_all(produced, "expert", split_axis=0, concat_axis=0, tiled=True)
    carried = (
        returned,
        arrived,
        hidden.reshape(groups * local_count, slot_count, hidden.shape[-1]),
    )
    returned = carried[0]
    combined = jnp.take(
        returned.reshape(experts * capacity, model_width), slot_ids, axis=0
    ).reshape(tokens, choices, model_width)
    mixture = jnp.sum(gating[:, :, None] * combined.astype(jnp.float32), axis=1)
    outputs = between_sections + mixture
    retained_values = (
        current,
        normed,
        queries,
        key_rows,
        value_rows,
        log_total,
        attended,
        between_sections,
        routed,
        logits,
        gating,
        slot_ids,
        source,
        filled,
        combined,
        carried[1:],
    )
    return (outputs, retained_values)


def layer_backward(grad_seed, retained_values, route_ids, weights):
    (
        qkv_weight,
        query_bias,
        value_bias,
        proj_weight,
        proj_bias,
        attn_gain,
        ffn_gain,
        router_weight,
        in_weight,
        out_weight,
    ) = weights
    (
        current,
        normed,
        queries,
        key_rows,
        value_rows,
        log_total,
        attended,
        between_sections,
        routed,
        logits,
        gating,
        slot_ids,
        source,
        filled,
        combined,
        kept_data,
    ) = retained_values
    tokens, model_width = grad_seed.shape
    choices = route_ids.shape[1]
    experts = router_weight.shape[1]
    capacity = capacity_of(tokens, choices, experts)
    groups = lax.axis_size("expert")
    local_count = in_weight.shape[0]
    grad_gating = jnp.sum(grad_seed[:, None, :] * combined.astype(jnp.float32), axis=-1)
    grad_rows = (
        (gating[:, :, None] * grad_seed[:, None, :])
        .astype(jnp.bfloat16)
        .reshape(tokens * choices, model_width)
    )
    outgoing = pack_rows(grad_rows, source, filled, experts, capacity)
    arriving = lax.all_to_all(outgoing, "expert", split_axis=0, concat_axis=0, tiled=True)
    row_data = kept_data[0].reshape(groups, local_count, capacity, model_width)
    hidden = kept_data[1].reshape(groups, local_count, capacity, kept_data[1].shape[-1])
    grad_out_rows = arriving.reshape(groups, local_count, capacity, model_width)
    active, gelu_back = jax.vjp(jax.nn.gelu, hidden)
    grad_wout = jnp.einsum(
        "necf,necd->efd",
        active.astype(jnp.bfloat16),
        grad_out_rows,
        preferred_element_type=jnp.float32,
    )
    grad_active = jnp.einsum(
        "necd,efd->necf", grad_out_rows, out_weight, preferred_element_type=jnp.float32
    )
    grad_hidden = gelu_back(grad_active)[0].astype(jnp.bfloat16)
    grad_win = jnp.einsum(
        "necd,necf->edf", row_data, grad_hidden, preferred_element_type=jnp.float32
    )
    grad_back_rows = jnp.einsum(
        "necf,edf->necd", grad_hidden, in_weight, preferred_element_type=jnp.float32
    )
    grad_back_rows = grad_back_rows.astype(jnp.bfloat16).reshape(experts, capacity, model_width)
    returning = lax.all_to_all(grad_back_rows, "expert", split_axis=0, concat_axis=0, tiled=True)
    gathered = jnp.take(returning.reshape(experts * capacity, model_width), slot_ids, axis=0)
    grad_routed = jnp.sum(
        gathered.astype(jnp.float32).reshape(tokens, choices, model_width), axis=1
    )
    choose = one_hot_ids(route_ids, experts)
    gate_back = jax.vjp(lambda scores: router_gates(scores, choose), logits)[1]
    grad_logits = gate_back(grad_gating)[0]
    grad_router = jnp.dot(
        routed.astype(jnp.float32).T, grad_logits, precision=lax.Precision.HIGHEST
    )
    grad_routed = grad_routed + jnp.dot(
        grad_logits, router_weight.astype(jnp.float32).T, precision=lax.Precision.HIGHEST
    )
    ffn_back = jax.vjp(norm_apply, between_sections, ffn_gain)[1]
    grad_middle, grad_gain_ffn = ffn_back(grad_routed)
    grad_middle = grad_middle + grad_seed
    grad_branch = grad_middle.astype(jnp.bfloat16)
    grad_pbias = jnp.sum(grad_branch.astype(jnp.float32), axis=0)
    grad_proj = jnp.dot(attended.T, grad_branch, preferred_element_type=jnp.float32)
    grad_attended = jnp.dot(grad_branch, proj_weight.T, preferred_element_type=jnp.float32).astype(
        jnp.bfloat16
    )
    grid_shape = (tokens // SEQ, SEQ, model_width // HD, HD)
    grad_query, grad_key, grad_value = lax.map(
        attend_backward,
        (
            queries.reshape(grid_shape),
            key_rows.reshape(grid_shape),
            value_rows.reshape(grid_shape),
            log_total,
            grad_attended.reshape(grid_shape),
        ),
    )
    grad_query = grad_query.reshape(tokens, model_width).astype(jnp.bfloat16)
    grad_key = grad_key.reshape(tokens, model_width).astype(jnp.bfloat16)
    grad_value = grad_value.reshape(tokens, model_width).astype(jnp.bfloat16)
    grad_packed = jnp.concatenate([grad_query, grad_key, grad_value], axis=1)
    grad_qbias = jnp.sum(grad_query.astype(jnp.float32), axis=0)
    grad_vbias = jnp.sum(grad_value.astype(jnp.float32), axis=0)
    grad_qkv = jnp.dot(normed.T, grad_packed, preferred_element_type=jnp.float32)
    grad_normed = jnp.dot(grad_packed, qkv_weight.T, preferred_element_type=jnp.float32)
    attn_back = jax.vjp(norm_apply, current, attn_gain)[1]
    grad_current, grad_gain_attn = attn_back(grad_normed)
    grad_current = grad_current + grad_middle
    shared = (
        grad_qkv,
        grad_qbias,
        grad_vbias,
        grad_proj,
        grad_pbias,
        grad_gain_attn,
        grad_gain_ffn,
        grad_router,
    )
    return (grad_current, shared, grad_win, grad_wout)


def relay_run(block_input, cotangent, expert_ids, weights):
    in_weight = weights[8]
    out_weight = weights[9]
    microbatch_count = block_input.shape[0]
    is_first = lax.axis_index("section") == 0
    own_ids = lax.dynamic_index_in_dim(expert_ids, lax.axis_index("section"), 0, keepdims=False)
    waiting = jnp.zeros(block_input.shape[1:], jnp.bfloat16)
    finished = []
    saved_activations = []
    for clock_step_index in range(microbatch_count + 1):
        own_rows = block_input[min(clock_step_index, microbatch_count - 1)]
        current = jnp.where(is_first, own_rows, waiting).astype(jnp.float32)
        routing_choices = jnp.where(
            is_first,
            own_ids[min(clock_step_index, microbatch_count - 1)],
            own_ids[max(clock_step_index - 1, 0)],
        )
        result, retained_values = layer_forward(current, routing_choices, weights)
        rounded = result.astype(jnp.bfloat16)
        finished.append(rounded)
        saved_activations.append((routing_choices, retained_values))
        if clock_step_index < microbatch_count:
            waiting = shifted(rounded, "section", 1)
    incoming = jnp.zeros(block_input.shape[1:], jnp.bfloat16)
    totals = None
    win_total = jnp.zeros(in_weight.shape, jnp.float32)
    wout_total = jnp.zeros(out_weight.shape, jnp.float32)
    record = []
    for clock_step_index in range(microbatch_count + 1):
        grad_seed = jnp.where(
            is_first,
            incoming.astype(jnp.float32),
            cotangent[min(clock_step_index, microbatch_count - 1)].astype(jnp.float32),
        )
        routing_choices, retained_values = jax.tree.map(
            lambda early, later: jnp.where(is_first, early, later),
            saved_activations[max(clock_step_index - 1, 0)],
            saved_activations[min(clock_step_index + 1, microbatch_count)],
        )
        live_mask = jnp.where(
            is_first,
            jnp.float32(clock_step_index >= 1),
            jnp.float32(clock_step_index < microbatch_count),
        )
        grad_current, shared, grad_win, grad_wout = layer_backward(
            grad_seed, retained_values, routing_choices, weights
        )
        shared = tuple((live_mask * term for term in shared))
        shared = lax.psum(shared, "expert")
        if totals is None:
            totals = shared
        else:
            totals = tuple((older + newer for older, newer in zip(totals, shared)))
        win_total = win_total + live_mask * grad_win
        wout_total = wout_total + live_mask * grad_wout
        sent_grad = grad_current.astype(jnp.bfloat16)
        record.append((grad_current, sent_grad))
        if clock_step_index < microbatch_count:
            incoming = shifted(sent_grad, "section", -1)
    section_out = jnp.stack(
        [
            jnp.where(is_first, finished[index_m], finished[index_m + 1])
            for index_m in range(microbatch_count)
        ]
    )
    section_grad = jnp.stack(
        [
            jnp.where(is_first, record[index_m + 1][0], record[index_m][1].astype(jnp.float32))
            for index_m in range(microbatch_count)
        ]
    )
    return (
        (section_out[None], section_grad[None])
        + tuple((term[None] for term in totals))
        + (win_total.astype(jnp.bfloat16)[None], wout_total.astype(jnp.bfloat16)[None])
    )


def shards(
    block_input,
    cotangent,
    expert_ids,
    qkv_weight,
    query_bias,
    value_bias,
    proj_weight,
    proj_bias,
    attn_gain,
    ffn_gain,
    router_weight,
    in_weight,
    out_weight,
):
    weights = (
        qkv_weight[0],
        query_bias[0],
        value_bias[0],
        proj_weight[0],
        proj_bias[0],
        attn_gain[0],
        ffn_gain[0],
        router_weight[0],
        in_weight[0],
        out_weight[0],
    )
    return relay_run(block_input, cotangent, expert_ids, weights)


def solution(mesh):
    return jax.shard_map(
        shards,
        mesh=mesh,
        in_specs=(
            P(None, "expert", None),
            P(None, "expert", None),
            P(None, None, "expert", None),
            P("section", None, None),
            P("section", None),
            P("section", None),
            P("section", None, None),
            P("section", None),
            P("section", None),
            P("section", None),
            P("section", None, None),
            P("section", "expert", None, None),
            P("section", "expert", None, None),
        ),
        out_specs=(
            P("section", None, "expert", None),
            P("section", None, "expert", None),
            P("section", None, None),
            P("section", None),
            P("section", None),
            P("section", None, None),
            P("section", None),
            P("section", None),
            P("section", None),
            P("section", None, None),
            P("section", "expert", None, None),
            P("section", "expert", None, None),
        ),
        check_vma=False,
    )
```

profile of v0, /device:TPU:0, one launch (start us, length us, event | category | flops | bytes accessed | tf_op | source)
XLA Modules:
  0.0 1694.9 jit_solution(12473064919775942904)
XLA Ops:
  178.5 51.1 %all_to_all.60 = bf16[16,68,768]{2,1,0:T(8,128)(2,1)S(1)} all-to-all(bf16[16,68,768]{2,1,0:T(8,128)(2,1)} %reshape.1132), channel_id=1, replica_groups=mesh['section'=2,'expert'=16] {'expert'}, dimensions={0} | all-to-all | bytes 3342336 | tf_op jit(solution)/shard_map/all_to_all | solution.py:139
  266.4 28.0 %all-to-all-done.1 = bf16[16,68,768]{2,1,0:T(8,128)(2,1)} async-done(((bf16[16,68,768]{2,1,0:T(8,128)(2,1)}), bf16[16,68,768]{2,1,0:T(8,128)(2,1)}, u32[]{:S(2)}, u32[]{:S(2)}) %all-to-all-start.1) | async-done | bytes 1671200 | tf_op jit(solution)/shard_map/all_to_all | solution.py:148
  313.7 16.3 multiply_reduce_fusion.8
  378.4 51.2 %all_to_all.61 = bf16[16,68,768]{2,1,0:T(8,128)(2,1)S(1)} all-to-all(bf16[16,68,768]{2,1,0:T(8,128)(2,1)} %reshape.1139), channel_id=1, replica_groups=mesh['section'=2,'expert'=16] {'expert'}, dimensions={0} | all-to-all | bytes 3342336 | tf_op jit(solution)/shard_map/all_to_all | solution.py:139
  443.6 12.0 fusion.182
  478.7 18.1 %all-to-all-done.3 = bf16[16,68,768]{2,1,0:T(8,128)(2,1)} async-done(((bf16[16,68,768]{2,1,0:T(8,128)(2,1)}), bf16[16,68,768]{2,1,0:T(8,128)(2,1)}, u32[]{:S(2)}, u32[]{:S(2)}) %all-to-all-start.3) | async-done | bytes 1671200 | tf_op jit(solution)/shard_map/all_to_all | solution.py:148
  547.8 24.4 %all-to-all-done.6 = bf16[16,68,768]{2,1,0:T(8,128)(2,1)} async-done(((bf16[16,68,768]{2,1,0:T(8,128)(2,1)}), bf16[16,68,768]{2,1,0:T(8,128)(2,1)}, u32[]{:S(2)}, u32[]{:S(2)}) %all-to-all-start.6) | async-done | bytes 1671200 | tf_op jit(solution)/shard_map/all_to_all | solution.py:225
  572.1 23.5 %fusion.6 = bf16[16,1,68,3072]{3,2,0,1:T(8,128)(2,1)} fusion(f32[16,68,3072]{2,1,0:T(8,128)} %copy-done.189, f32[16,68,3072]{2,1,0:T(8,128)} %copy-done.188, pred[]{:T(512)S(6)} %eq.150, bf16[16,68,768]{2,1,0:T(8,128)(2,1)} %all-to-all-done.6, bf16[1,1,3072,768]{3,2,1,0:T(8,128)(2,1)} %param.31), kind=kOutput, calls=%fused_computation.33 | convolution fusion | flops 5204017152 | bytes 39813120 | tf_op jit(solution)/shard_map/necd,efd->necf/dot_general | solution.py:236
  634.1 16.4 multiply_reduce_fusion.7
  696.8 13.7 multiply_reduce_fusion.2
  774.5 48.3 %all_to_all.62 = bf16[16,68,768]{2,1,0:T(8,128)(2,1)S(1)} all-to-all(bf16[16,68,768]{2,1,0:T(8,128)(2,1)} %reshape.1144), channel_id=1, replica_groups=mesh['section'=2,'expert'=16] {'expert'}, dimensions={0} | all-to-all | bytes 3342336 | tf_op jit(solution)/shard_map/all_to_all | solution.py:139
  836.7 12.0 fusion.187
  965.1 23.5 %fusion.13 = bf16[16,1,68,3072]{3,2,0,1:T(8,128)(2,1)} fusion(f32[16,68,3072]{2,1,0:T(8,128)} %copy-done.190, f32[16,68,3072]{2,1,0:T(8,128)} %copy-done.188, pred[]{:T(512)S(6)} %eq.150, bf16[16,68,768]{2,1,0:T(8,128)(2,1)} %all-to-all-done.8, bf16[1,1,3072,768]{3,2,1,0:T(8,128)(2,1)} %param.31), kind=kOutput, calls=%fused_computation.40 | convolution fusion | flops 5204017152 | bytes 39813120 | tf_op jit(solution)/shard_map/necd,efd->necf/dot_general | solution.py:236
  1092.6 11.2 multiply_reduce_fusion.1
  1124.1 16.9 fusion.66
  1177.7 12.1 fusion.74
  1194.9 16.7 multiply_reduce_fusion.6
  1230.8 23.5 %fusion.20 = bf16[16,1,68,3072]{3,2,0,1:T(8,128)(2,1)} fusion(f32[16,68,3072]{2,1,0:T(8,128)} %copy-done.190, f32[16,68,3072]{2,1,0:T(8,128)} %copy-done.189, pred[]{:T(512)S(6)} %eq.150, bf16[16,68,768]{2,1,0:T(8,128)(2,1)} %all-to-all-done.10, bf16[1,1,3072,768]{3,2,1,0:T(8,128)(2,1)} %param.31), kind=kOutput, calls=%fused_computation.47 | convolution fusion | flops 5204017152 | bytes 39813120 | tf_op jit(solution)/shard_map/necd,efd->necf/dot_general | solution.py:236
  1271.9 16.9 fusion.64
  1288.8 11.8 fusion.70
  1392.9 15.0 fusion.145
  1407.9 21.8 %fusion.126 = bf16[1,1,3072,768]{3,2,1,0:T(8,128)(2,1)} fusion(f32[3072,768,1]{1,0,2:T(8,128)} %fusion.64, f32[3072,768,1]{1,0,2:T(8,128)} %fusion.66, f32[]{:T(128)S(6)} %select_n.629, f32[]{:T(128)S(6)} %select_n.626, bf16[16,68,768]{2,1,0:T(8,128)(2,1)} %all-to-all-done.6, f32[16,68,3072]{2,1,0:T(8,128)} %copy-done.189, ...), kind=kOutput, calls=%fused_computation.182 | convolution fusion | flops 5179047936 | bytes 52002824 | tf_op jit(solution)/shard_map/necf,necd->efd/dot_general | solution.py:230
  1442.2 84.5 %all-reduce = (f32[768]{0:T(1024)}, f32[768]{0:T(1024)}, f32[768]{0:T(1024)}, f32[768]{0:T(1024)}, f32[768]{0:T(1024)}, /*index=5*/f32[768,16]{0,1:T(8,128)}) all-reduce(f32[768]{0:T(1024)S(1)} %copy-done.156, f32[768]{0:T(1024)S(1)} %copy-done.157, ...), channel_id=1, replica_groups=mesh['section'=2,'expert'=16] {'expert'}, use_global_device_ids=true, to_apply=%region_88.92 | all-reduce | flops 16128 | bytes 129024 | tf_op jit(solution)/shard_map/psum | solution.py:353
  1538.9 141.0 %all-reduce.4.cloned.1.call-done = (f32[768,2304]{1,0:T(8,128)}, f32[768,768]{1,0:T(8,128)}) async-done(((f32[768,2304]{1,0:T(8,128)}, f32[768,768]{1,0:T(8,128)}), (f32[768,2304]{1,0:T(8,128)}, f32[768,768]{1,0:T(8,128)})) %all-reduce.4.cloned.1.call-update) | async-done | bytes 9437200 | tf_op jit(solution)/shard_map/psum | solution.py:353
  (771 shorter events, 968.7 us)
Async XLA Ops:
  9.6 19.1 %copy-start.114 = (s32[1,1,512,2]{2,3,1,0:T(2,128)}, s32[1,1,512,2]{2,3,1,0:T(2,128)S(1)}, u32[]{:S(2)}) copy-start(s32[1,1,512,2]{2,3,1,0:T(2,128)S(1)} %get-tuple-element.204) | copy-start | bytes 12292
  21.4 313.3 %copy-start.111 = (f32[768]{0:T(1024)}, f32[768]{0:T(1024)S(1)}, u32[]{:S(2)}) copy-start(f32[768]{0:T(1024)S(1)} %reduce.21) | copy-start | bytes 9220
  24.1 313.6 %copy-start.117 = (f32[768]{0:T(1024)}, f32[768]{0:T(1024)S(1)}, u32[]{:S(2)}) copy-start(f32[768]{0:T(1024)S(1)} %reduce.23) | copy-start | bytes 9220
  39.2 1038.4 %copy-start.103 = (f32[768]{0:T(1024)}, f32[768]{0:T(1024)S(1)}, u32[]{:S(2)}) copy-start(f32[768]{0:T(1024)S(1)} %reduce.25) | copy-start | bytes 9220
  178.5 65.0 %slice-start.11 = ((s8[4718592]{0:T(1024)(128)(4,1)}), s8[4194304]{0:T(1024)(128)(4,1)S(1)}, s32[]{:S(2)}) async-start(s8[4718592]{0:T(1024)(128)(4,1)} %bitcast.666), calls=%async_computation.24 | async-start | bytes 8388608
  253.1 41.2 %all-to-all-start.1 = ((bf16[16,68,768]{2,1,0:T(8,128)(2,1)}), bf16[16,68,768]{2,1,0:T(8,128)(2,1)}, u32[]{:S(2)}, u32[]{:S(2)}) async-start(bf16[16,68,768]{2,1,0:T(8,128)(2,1)} %fusion.177), calls=%async_computation.1 | async-start | bytes 3538944 | tf_op jit(solution)/shard_map/all_to_all | solution.py:148
  330.3 3.3 collective-permute-start
  455.6 41.3 %all-to-all-start.3 = ((bf16[16,68,768]{2,1,0:T(8,128)(2,1)}), bf16[16,68,768]{2,1,0:T(8,128)(2,1)}, u32[]{:S(2)}, u32[]{:S(2)}) async-start(bf16[16,68,768]{2,1,0:T(8,128)(2,1)} %fusion.182), calls=%async_computation.3 | async-start | bytes 3538944 | tf_op jit(solution)/shard_map/all_to_all | solution.py:148
  476.1 60.4 %copy-start.127 = (f32[512,2]{0,1:T(2,128)}, f32[512,2]{0,1:T(2,128)S(1)}, u32[]{:S(2)}) copy-start(f32[512,2]{0,1:T(2,128)S(1)} %get-tuple-element.241) | copy-start | bytes 12292
  526.8 45.4 %all-to-all-start.6 = ((bf16[16,68,768]{2,1,0:T(8,128)(2,1)}), bf16[16,68,768]{2,1,0:T(8,128)(2,1)}, u32[]{:S(2)}, u32[]{:S(2)}) async-start(bf16[16,68,768]{2,1,0:T(8,128)(2,1)} %reshape.1147), calls=%async_computation.6 | async-start | bytes 3538944 | tf_op jit(solution)/shard_map/all_to_all | solution.py:225
  605.9 54.3 %all-to-all-start.7 = ((bf16[16,68,768]{2,1,0:T(8,128)(2,1)}), bf16[16,68,768]{2,1,0:T(8,128)(2,1)}, u32[]{:S(2)}, u32[]{:S(2)}) async-start(bf16[16,68,768]{2,1,0:T(8,128)(2,1)} %fusion.192), calls=%async_computation.7 | async-start | bytes 3538944 | tf_op jit(solution)/shard_map/all_to_all | solution.py:247
  652.0 74.7 %collective-permute-start.1 = (bf16[512,768]{1,0:T(8,128)(2,1)}, bf16[512,768]{1,0:T(8,128)(2,1)}, u32[]{:S(2)}, u32[]{:S(2)}) collective-permute-start(bf16[512,768]{1,0:T(8,128)(2,1)} %get-tuple-element.224), channel_id=1, source_target_pairs={{0,16},{1,17},{2,18},{3,19},{4,20},{5,21},{6,22},{7,23},{8,24},{9,... | collective-permute-start | bytes 2359304 | tf_op jit(solution)/shard_map/ppermute | solution.py:17
  848.7 40.6 %all-to-all-start.5 = ((bf16[16,68,768]{2,1,0:T(8,128)(2,1)}), bf16[16,68,768]{2,1,0:T(8,128)(2,1)}, u32[]{:S(2)}, u32[]{:S(2)}) async-start(bf16[16,68,768]{2,1,0:T(8,128)(2,1)} %fusion.187), calls=%async_computation.5 | async-start | bytes 3538944 | tf_op jit(solution)/shard_map/all_to_all | solution.py:148
  869.5 9.0 collective-permute-start.2
  918.8 46.3 %all-to-all-start.8 = ((bf16[16,68,768]{2,1,0:T(8,128)(2,1)}), bf16[16,68,768]{2,1,0:T(8,128)(2,1)}, u32[]{:S(2)}, u32[]{:S(2)}) async-start(bf16[16,68,768]{2,1,0:T(8,128)(2,1)} %reshape.1152), calls=%async_computation.8 | async-start | bytes 3538944 | tf_op jit(solution)/shard_map/all_to_all | solution.py:225
  998.8 47.2 %all-to-all-start.9 = ((bf16[16,68,768]{2,1,0:T(8,128)(2,1)}), bf16[16,68,768]{2,1,0:T(8,128)(2,1)}, u32[]{:S(2)}, u32[]{:S(2)}) async-start(bf16[16,68,768]{2,1,0:T(8,128)(2,1)} %fusion.197), calls=%async_computation.9 | async-start | bytes 3538944 | tf_op jit(solution)/shard_map/all_to_all | solution.py:247
  1092.6 24.0 %copy-start.186 = (bf16[12,64,512]{2,1,0:T(8,128)(2,1)}, bf16[12,64,512]{2,1,0:T(8,128)(2,1)S(1)}, u32[]{:S(2)}) copy-start(bf16[12,64,512]{2,1,0:T(8,128)(2,1)S(1)} %get-tuple-element.342) | copy-start | bytes 2359300
  1122.6 18.3 %copy-start.64 = (bf16[2,512,768]{2,1,0:T(8,128)(2,1)S(1)}, bf16[2,512,768]{2,1,0:T(8,128)(2,1)}, u32[]{:S(2)}) copy-start(bf16[2,512,768]{2,1,0:T(8,128)(2,1)} %param.20) | copy-start | bytes 4718596
  1122.6 18.3 %collective-permute-start.3 = (bf16[512,768]{1,0:T(8,128)(2,1)S(1)}, bf16[512,768]{1,0:T(8,128)(2,1)S(1)}, u32[]{:S(2)}, u32[]{:S(2)}) collective-permute-start(bf16[512,768]{1,0:T(8,128)(2,1)S(1)} %get-tuple-element.194), channel_id=1, source_target_pairs={{16,0},{17,1},{18,2},{19,3},{20,4},{21,5},{22,6},{23,7},{24,8},{25... | collective-permute-start | bytes 2359304 | tf_op jit(solution)/shard_map/ppermute | solution.py:17
  1169.2 61.6 %all-to-all-start.10 = ((bf16[16,68,768]{2,1,0:T(8,128)(2,1)}), bf16[16,68,768]{2,1,0:T(8,128)(2,1)}, u32[]{:S(2)}, u32[]{:S(2)}) async-start(bf16[16,68,768]{2,1,0:T(8,128)(2,1)} %reshape.1157), calls=%async_computation.10 | async-start | bytes 3538944 | tf_op jit(solution)/shard_map/all_to_all | solution.py:225
  1264.8 44.7 %all-to-all-start.11 = ((bf16[16,68,768]{2,1,0:T(8,128)(2,1)}), bf16[16,68,768]{2,1,0:T(8,128)(2,1)}, u32[]{:S(2)}, u32[]{:S(2)}) async-start(bf16[16,68,768]{2,1,0:T(8,128)(2,1)} %fusion.202), calls=%async_computation.11 | async-start | bytes 3538944 | tf_op jit(solution)/shard_map/all_to_all | solution.py:247
  1271.8 408.1 %all-reduce.4.cloned.1.call-start = ((), (), s32[]{:S(2)}) async-start(), calls=%async_computation.12 | async-start | bytes 18874368 | tf_op jit(solution)/shard_map/psum | solution.py:353
  1407.9 21.8 %copy-start.133 = (f32[12,64]{1,0:T(8,128)S(1)}, f32[12,64]{1,0:T(8,128)}, u32[]{:S(2)}) copy-start(f32[12,64]{1,0:T(8,128)} %get-tuple-element.339) | copy-start | bytes 9220
  1407.9 25.9 %copy-start.155 = (f32[768]{0:T(1024)S(1)}, f32[768]{0:T(1024)}, u32[]{:S(2)}) copy-start(f32[768]{0:T(1024)} %get-tuple-element.187) | copy-start | bytes 9220
  (194 other events, 1024.5 us)
Sparse Core Ops, SparseCore 0:
  1393.0 286.8 all-reduce.3
where the time goes:
time: 1710 us; the launch traced here: 1690 us
  matrix products  452 us (26%)
  local copies, waits for them, and re-layouts  385 us (23%)
  other arithmetic  308 us (18%)
  blocking collectives  235 us (14%)
  waiting for transfers between devices  227 us (13%)
  starting transfers between devices  71.5 us (4%)
    all_to_all x3, blocking collectives, layer_forward(): lax.all_to_all(sending, 'expert', split_axis=0, concat_axis=0, tiled=True)  151 us
    psum x1, waiting for transfers between devices, relay_run(): shared = lax.psum(shared, 'expert')  141 us
    psum x1, blocking collectives, relay_run(): shared = lax.psum(shared, 'expert')  84.5 us
    dot_general x3, matrix products, layer_backward(): jnp.einsum('necd,efd->necf', grad_out_rows, out_weight, preferred_element...  70.5 us
    dot_general x3, matrix products, layer_backward(): jnp.einsum('necf,necd->efd', active.astype(jnp.bfloat16), grad_out_rows,...  55.6 us
    reduce_sum x3, other arithmetic, layer_forward(): mixture = jnp.sum(gating[:, :, None] * combined.astype(jnp.float32), axis=1)  49.5 us
    unnamed x410, local copies, waits for them, and re-layouts  48.2 us
    all_to_all x3, waiting for transfers between devices, layer_forward(): lax.all_to_all(produced, 'expert', split_axis=0, concat_axis=0, tiled=True)  46.1 us
  transfers between devices with their start and end apart: 14, of which 9 were waited for; matrix products, arithmetic and copies ran while one was open for 24% of the time, Pallas kernels for 0%

commit v1 on v0

v1 whole, which is shorter than its diff:
```python
import jax
import jax.numpy as jnp
from jax import lax
from jax.sharding import PartitionSpec as P

HD = 64
EPS = 1e-06
NEG = -1e30
BF = jnp.bfloat16
F32 = jnp.float32
HIGH = lax.Precision.HIGHEST
SWAP = [(0, 1), (1, 0)]


def dot(a, b, dims, kind=F32, precision=None):
    return lax.dot_general(
        a, b, (dims, ((), ())), precision=precision, preferred_element_type=F32
    ).astype(kind)


NN = ((1,), (0,))
NT = ((1,), (1,))
TN = ((0,), (0,))


def capacity_of(tokens, choices, experts):
    return tokens * choices // experts + max(1, tokens * choices // (16 * experts))


def inverse_rms(field):
    return lax.rsqrt(jnp.mean(field * field, axis=-1, keepdims=True) + EPS)


def norm_back(field, gain, grad):
    scale = inverse_rms(field)
    unit = field * scale
    grad_gain = jnp.sum(grad * unit, axis=0)
    scaled = grad * gain
    grad_field = scale * (scaled - unit * jnp.mean(scaled * unit, axis=-1, keepdims=True))
    return grad_field, grad_gain


def causal_scores(queries, key_rows):
    scores = jnp.einsum(
        "qhd,khd->hqk", queries, key_rows, preferred_element_type=F32
    ) * HD ** (-0.5)
    length = scores.shape[-1]
    causal = jnp.arange(length)[:, None] >= jnp.arange(length)[None, :]
    return jnp.where(causal[None], scores, NEG)


def attend_forward(queries, key_rows, value_rows):
    tokens, width = queries.shape
    shape = (tokens, width // HD, HD)
    scores = causal_scores(queries.reshape(shape), key_rows.reshape(shape))
    row_max = jnp.max(scores, axis=-1, keepdims=True)
    weights = jnp.exp(scores - row_max)
    row_total = jnp.sum(weights, axis=-1, keepdims=True)
    prob_low = (weights / row_total).astype(BF)
    attended = jnp.einsum(
        "hqk,khd->qhd", prob_low, value_rows.reshape(shape), preferred_element_type=F32
    )
    return (
        attended.astype(BF).reshape(tokens, width),
        row_max[..., 0] + jnp.log(row_total[..., 0]),
    )


def attend_backward(queries, key_rows, value_rows, log_total, grad_out):
    tokens, width = queries.shape
    shape = (tokens, width // HD, HD)
    queries, key_rows, value_rows, grad_out = (
        part.reshape(shape) for part in (queries, key_rows, value_rows, grad_out)
    )
    scores = causal_scores(queries, key_rows)
    weights = jnp.exp(scores - log_total[..., None])
    grad_probs = jnp.einsum("qhd,khd->hqk", grad_out, value_rows, preferred_element_type=F32)
    inner = jnp.sum(weights * grad_probs, axis=-1, keepdims=True)
    grad_scores = (weights * (grad_probs - inner)).astype(BF)
    grad_value = jnp.einsum(
        "hqk,qhd->khd", weights.astype(BF), grad_out, preferred_element_type=F32
    )
    grad_query = jnp.einsum(
        "hqk,khd->qhd", grad_scores, key_rows, preferred_element_type=F32
    ) * HD ** (-0.5)
    grad_key = jnp.einsum(
        "hqk,qhd->khd", grad_scores, queries, preferred_element_type=F32
    ) * HD ** (-0.5)
    return tuple(
        part.astype(BF).reshape(tokens, width) for part in (grad_query, grad_key, grad_value)
    )


def gelu_and_slope(hidden):
    root = 0.7978845608028654
    square = hidden * hidden
    bent = jnp.tanh(root * hidden * (1.0 + 0.044715 * square))
    half = 0.5 * (1.0 + bent)
    slope = half + 0.5 * hidden * (1.0 - bent * bent) * root * (1.0 + 0.134145 * square)
    return hidden * half, slope


def route_plan(route_ids, experts, capacity):
    tokens = route_ids.shape[0]
    lanes = jnp.arange(experts, dtype=jnp.int32)[None, :]
    first = (route_ids[:, 0:1] == lanes).astype(F32)
    second = (route_ids[:, 1:2] == lanes).astype(F32)
    places = jnp.arange(tokens, dtype=jnp.int32)
    earlier = (places[:, None] > places[None, :]).astype(BF)
    counts = dot(earlier, (first + second).astype(BF), NN)
    ranks = [jnp.sum(counts * hot, axis=-1).astype(jnp.int32) for hot in (first, second)]
    slots = [route_ids[:, j] * capacity + ranks[j] for j in range(2)]
    row = jnp.arange(experts * capacity, dtype=jnp.int32)[:, None]
    place = [(row == slot[None, :]).astype(BF) for slot in slots]
    return first, second, place[0], place[1]


def exchange(rows, experts):
    total, width = rows.shape
    moved = lax.all_to_all(
        rows.reshape(experts, total // experts, width),
        "expert",
        split_axis=0,
        concat_axis=0,
        tiled=True,
    )
    return moved.reshape(total, width)


def layer_forward(current, plan, weights):
    qkv, qbias, vbias, proj, pbias, gain_attn, gain_ffn, router, win, wout = weights
    first, second, place0, place1 = plan
    width = current.shape[1]
    experts = router.shape[1]
    normed = (current * inverse_rms(current) * gain_attn).astype(BF)
    packed = dot(normed, qkv, NN)
    queries = (packed[:, :width] + qbias).astype(BF)
    key_rows = packed[:, width : 2 * width].astype(BF)
    value_rows = (packed[:, 2 * width :] + vbias).astype(BF)
    attended, log_total = attend_forward(queries, key_rows, value_rows)
    middle = current + (dot(attended, proj, NN) + pbias)
    routed = (middle * inverse_rms(middle) * gain_ffn).astype(BF)
    logits = dot(routed, router, NN)
    gap = jnp.sum(logits * (first - second), axis=-1, keepdims=True)
    gate0, gate1 = jax.nn.sigmoid(gap), jax.nn.sigmoid(-gap)
    arrived = exchange(dot(place0 + place1, routed, NN, BF), experts)
    hidden = dot(arrived, win, NN)
    active, slope = gelu_and_slope(hidden)
    active, slope = active.astype(BF), slope.astype(BF)
    produced = dot(active, wout, NN, BF)
    returned = exchange(produced, experts)
    combined0 = dot(place0, returned, TN, BF)
    combined1 = dot(place1, returned, TN, BF)
    outputs = middle + (gate0 * combined0.astype(F32) + gate1 * combined1.astype(F32))
    kept = (
        current, normed, queries, key_rows, value_rows, log_total, attended, middle, routed,
        gate0, gate1, combined0, combined1, arrived, active, slope,
    )
    return outputs, kept


def layer_backward(seed, kept, plan, weights):
    qkv, qbias, vbias, proj, pbias, gain_attn, gain_ffn, router, win, wout = weights
    first, second, place0, place1 = plan
    (
        current, normed, queries, key_rows, value_rows, log_total, attended, middle, routed,
        gate0, gate1, combined0, combined1, arrived, active, slope,
    ) = kept
    experts = router.shape[1]
    outgoing = dot(place0, (gate0 * seed).astype(BF), NN) + dot(
        place1, (gate1 * seed).astype(BF), NN
    )
    arriving = exchange(outgoing.astype(BF), experts)
    grad_active = dot(arriving, wout, NT)
    grad_hidden = (grad_active * slope.astype(F32)).astype(BF)
    returning = exchange(dot(grad_hidden, win, NT, BF), experts)
    grad_wout = dot(active, arriving, TN, BF)
    grad_win = dot(arrived, grad_hidden, TN, BF)
    grad_gap = gate0 * gate1 * jnp.sum(
        seed * (combined0.astype(F32) - combined1.astype(F32)), axis=-1, keepdims=True
    )
    grad_logits = grad_gap * (first - second)
    grad_router = dot(grad_logits, routed.astype(F32), TN, precision=HIGH)
    grad_routed = dot(place0 + place1, returning, TN) + dot(
        grad_logits, router.astype(F32), NT, precision=HIGH
    )
    grad_middle, grad_gain_ffn = norm_back(middle, gain_ffn, grad_routed)
    grad_middle = grad_middle + seed
    grad_branch = grad_middle.astype(BF)
    grad_pbias = jnp.sum(grad_branch.astype(F32), axis=0)
    grad_proj = dot(attended, grad_branch, TN, BF)
    grad_attended = dot(grad_branch, proj, NT, BF)
    grad_query, grad_key, grad_value = attend_backward(
        queries, key_rows, value_rows, log_total, grad_attended
    )
    grad_packed = jnp.concatenate([grad_query, grad_key, grad_value], axis=1)
    grad_qbias = jnp.sum(grad_query.astype(F32), axis=0)
    grad_vbias = jnp.sum(grad_value.astype(F32), axis=0)
    grad_qkv = [dot(normed, part, TN, BF) for part in (grad_query, grad_key, grad_value)]
    grad_normed = dot(grad_packed, qkv, NT)
    grad_current, grad_gain_attn = norm_back(current, gain_attn, grad_normed)
    grad_current = grad_current + grad_middle
    small = jnp.concatenate(
        [
            jnp.stack([grad_qbias, grad_vbias, grad_pbias, grad_gain_attn, grad_gain_ffn]),
            grad_router,
        ]
    )
    small = jnp.pad(small, ((0, -small.shape[0] % 32), (0, 0)))
    shared = jnp.concatenate(grad_qkv + [grad_proj, small.astype(BF)])
    return grad_current, shared, grad_win, grad_wout


def reduce_shared(shared, section):
    half = shared.shape[0] // 2
    own = lax.dynamic_slice_in_dim(shared, section * half, half, 0)
    other = lax.dynamic_slice_in_dim(shared, (1 - section) * half, half, 0)
    other = lax.ppermute(other, "section", SWAP)
    return lax.psum((own.astype(F32) + other.astype(F32)).astype(BF), "expert")


def both(own, other, is_first):
    return jnp.where(is_first, own, other), jnp.where(is_first, other, own)


def shards(
    block_input, cotangent, expert_ids, qkv_weight, query_bias, value_bias, proj_weight,
    proj_bias, attn_gain, ffn_gain, router_weight, in_weight, out_weight,
):
    section = lax.axis_index("section")
    is_first = section == 0
    width = block_input.shape[2]
    experts = router_weight.shape[2]
    tokens = block_input.shape[1]
    capacity = capacity_of(tokens, expert_ids.shape[3], experts)

    def gathered(array):
        return lax.all_gather(array, "section", axis=0, tiled=True)

    vectors = gathered(
        jnp.stack([query_bias, value_bias, proj_bias, attn_gain, ffn_gain], axis=1)
    )
    qkv_all, proj_all, router_all = (
        gathered(part) for part in (qkv_weight, proj_weight, router_weight)
    )
    win_all, wout_all = gathered(in_weight), gathered(out_weight)
    layers = [
        (
            qkv_all[l], vectors[l, 0], vectors[l, 1], proj_all[l], vectors[l, 2], vectors[l, 3],
            vectors[l, 4], router_all[l], win_all[l, 0], wout_all[l, 0],
        )
        for l in range(2)
    ]
    rows = lax.dynamic_index_in_dim(block_input, section, 0, keepdims=False)
    seed = lax.dynamic_index_in_dim(cotangent, section, 0, keepdims=False)
    ids = lax.dynamic_index_in_dim(expert_ids, section, 1, keepdims=False)
    plans = [route_plan(ids[l], experts, capacity) for l in range(2)]

    out0, kept0 = layer_forward(rows.astype(F32), plans[0], layers[0])
    out0 = out0.astype(BF)
    out1, kept1 = layer_forward(out0.astype(F32), plans[1], layers[1])
    out1 = out1.astype(BF)
    out_other = lax.ppermute(jnp.where(is_first, out1, out0), "section", SWAP)
    section_out = jnp.stack(both(jnp.where(is_first, out0, out1), out_other, is_first))

    grad1, shared1, win1, wout1 = layer_backward(seed.astype(F32), kept1, plans[1], layers[1])
    grad1 = grad1.astype(BF)
    up, down = [(0, 1)], [(1, 0)]
    win1_other = lax.ppermute(win1, "section", up)
    wout1_other = lax.ppermute(wout1, "section", up)
    grad1_other = lax.ppermute(grad1, "section", up)
    total1 = reduce_shared(shared1, section)
    total1_other = lax.ppermute(total1, "section", up)

    grad0, shared0, win0, wout0 = layer_backward(grad1.astype(F32), kept0, plans[0], layers[0])
    win0_other = lax.ppermute(win0, "section", down)
    wout0_other = lax.ppermute(wout0, "section", down)
    grad0_other = lax.ppermute(grad0, "section", down)
    shared0, total1 = lax.optimization_barrier((shared0, total1))
    total0 = reduce_shared(shared0, section)
    total0_other = lax.ppermute(total0, "section", down)

    section_grad = jnp.stack(
        [
            jnp.where(is_first, grad0, grad1_other.astype(F32)),
            jnp.where(is_first, grad0_other, grad1.astype(F32)),
        ]
    )

    def summed(first, first_other, second, second_other):
        return jnp.where(
            is_first,
            first.astype(F32) + first_other.astype(F32),
            second.astype(F32) + second_other.astype(F32),
        ).astype(BF)

    grad_win = summed(win0, win0_other, win1, win1_other)
    grad_wout = summed(wout0, wout0_other, wout1, wout1_other)
    total = jnp.concatenate(
        [
            jnp.where(is_first, total0, total1_other),
            jnp.where(is_first, total0_other, total1),
        ]
    ).astype(F32)
    grad_qkv = jnp.concatenate([total[i * width : (i + 1) * width] for i in range(3)], axis=1)
    grad_proj = total[3 * width : 4 * width]
    small = total[4 * width : 4 * width + 5 + experts]
    return (
        section_out[None],
        section_grad[None],
        grad_qkv[None],
        small[0][None],
        small[1][None],
        grad_proj[None],
        small[2][None],
        small[3][None],
        small[4][None],
        small[5:].T[None],
        grad_win[None, None],
        grad_wout[None, None],
    )


def solution(mesh):
    vector, matrix = P("section", None), P("section", None, None)
    expert = P("section", "expert", None, None)
    rows = P("section", None, "expert", None)
    return jax.shard_map(
        shards,
        mesh=mesh,
        in_specs=(
            P(None, "expert", None),
            P(None, "expert", None),
            P(None, None, "expert", None),
            matrix, vector, vector, matrix, vector, vector, vector, matrix, expert, expert,
        ),
        out_specs=(
            rows, rows, matrix, vector, vector, matrix, vector, vector, vector, matrix,
            expert, expert,
        ),
        check_vma=False,
    )
```

time: 1710 us -> 998 us (0.58)
  local copies, waits for them, and re-layouts: 385 us -> 86.7 us
  other arithmetic: 308 us -> 79.3 us
  matrix products: 452 us -> 274 us
  waiting for transfers between devices: 227 us -> 322 us
  blocking collectives: 235 us -> 154 us
  starting transfers between devices: 71.5 us -> 53.3 us
    dot_general x63 -> x58, matrix products: 447 us -> 271 us  [the longest x48 209 us: dot(): lax.dot_general(a, b, (dims, ((), ())), precision=precision, preferred_el...]
    reduce_sum x40 -> x4, other arithmetic: 110 us -> 7.11 us  [the longest x2 4.5 us: layer_backward(): grad_pbias = jnp.sum(grad_branch.astype(F32), axis=0)]
    gather x12 -> x0, local copies, waits for them, and re-layouts: 88.4 us -> none  [the longest x6 43.9 us: pack_rows(): taken = jnp.take(row_data, source, axis=0)]
    psum x1 -> x0, blocking collectives: 84.5 us -> none  [relay_run(): shared = lax.psum(shared, 'expert')]
    psum x1 -> x2, waiting for transfers between devices: 141 us -> 185 us  [reduce_shared(): return lax.psum((own.astype(F32) + other.astype(F32)).astype(BF), 'expert')]
    select_n x25 -> x2, other arithmetic: 46 us -> 3.84 us  [the longest x1 1.93 us: shards(): jnp.where(is_first, total0_other, total1)]
    another operation x13 -> x3, other arithmetic: 44 us -> 4.75 us  [the longest x2 3.34 us: shards(): jnp.stack([jnp.where(is_first, grad0, grad1_other.astype(F32)), jnp.where...]
    convert_element_type x12 -> x6, local copies, waits for them, and re-layouts: 36 us -> 1.68 us  [the longest x2 0.56 us: layer_forward(): queries = (packed[:, :width] + qbias).astype(BF)]
  transfers between devices with their start and end apart: 14 -> 22, of which waited for: 9 -> 9; matrix products, arithmetic and copies ran while one was open for 24% -> 23% of each run, Pallas kernels for 0% -> 0%
where the time goes in v1:
time: 998 us; the launch traced here: 985 us
  waiting for transfers between devices  322 us (32%)
  matrix products  274 us (27%)
  blocking collectives  154 us (15%)
  local copies, waits for them, and re-layouts  86.7 us (9%)
  other arithmetic  79.3 us (8%)
  starting transfers between devices  53.3 us (5%)
  between operations  16.4 us (2%)
    dot_general x48, matrix products, dot(): lax.dot_general(a, b, (dims, ((), ())), precision=precision, preferred_el...  209 us
    psum x2, waiting for transfers between devices, reduce_shared(): return lax.psum((own.astype(F32) + other.astype(F32)).astype(BF), 'expert')  185 us
    all_to_all x3, blocking collectives, exchange(): lax.all_to_all(rows.reshape(experts, total // experts, width), 'expert',...  150 us
    all_to_all x5, waiting for transfers between devices, exchange(): lax.all_to_all(rows.reshape(experts, total // experts, width), 'expert',...  117 us
    all_to_all x5, starting transfers between devices, exchange(): lax.all_to_all(rows.reshape(experts, total // experts, width), 'expert',...  30.9 us
    reshape x8, local copies, waits for them, and re-layouts, exchange(): rows.reshape(experts, total // experts, width)  27.2 us
    reshape x8, local copies, waits for them, and re-layouts, exchange(): return moved.reshape(total, width)  23.1 us
    unnamed x278, local copies, waits for them, and re-layouts  22.7 us
  transfers between devices with their start and end apart: 22, of which 9 were waited for; matrix products, arithmetic and copies ran while one was open for 23% of the time, Pallas kernels for 0%

profile of v1, /device:TPU:0, one launch (start us, length us, event | category | flops | bytes accessed | tf_op | source)
XLA Modules:
  0.0 985.1 jit_solution(1497431920451466052)
XLA Ops:
  14.1 16.1 %all-gather.5.cloned.1.call-done = bf16[2,768,2304]{2,1,0:T(8,128)(2,1)} async-done(((bf16[1,768,2304]{2,1,0:T(8,128)(2,1)}), bf16[2,768,2304]{2,1,0:T(8,128)(2,1)}) %all-gather.5.cloned.1.call-update) | async-done | bytes 7077904 | tf_op jit(solution)/shard_map/all_gather | solution.py:238
  55.6 49.8 %all_to_all.40 = bf16[16,68,768]{2,1,0:T(8,128)(2,1)} all-to-all(bf16[16,68,768]{2,1,0:T(8,128)(2,1)} %reshape.378), channel_id=1, replica_groups=mesh['section'=2,'expert'=16] {'expert'}, dimensions={0} | all-to-all | bytes 3342336 | tf_op jit(solution)/shard_map/all_to_all | solution.py:120
  108.8 11.0 %fusion.19 = f32[1088,3072]{1,0:T(8,128)} fusion(bf16[1088,768]{1,0:T(8,128)(2,1)} %reshape.379, bf16[2,1,768,3072]{3,2,1,0:T(8,128)(2,1)} %all-gather.9.cloned.1.call-done), kind=kOutput, calls=%fused_computation.53 | convolution fusion | flops 5133828096 | bytes 19759104 | tf_op jit(solution)/shard_map/dot_general | solution.py:16
  119.8 13.0 %fusion.26 = bf16[1088,768]{1,0:T(8,128)(2,1)} fusion(bf16[2,1,3072,768]{3,2,1,0:T(8,128)(2,1)} %all-gather.11.cloned.1.call-done, f32[1088,3072]{1,0:T(8,128)} %fusion.19), kind=kOutput, calls=%fused_computation.64 | convolution fusion | flops 5164744704 | bytes 19759104 | tf_op jit(solution)/shard_map/dot_general | solution.py:16
  145.0 32.4 %all-to-all-done.1 = bf16[16,68,768]{2,1,0:T(8,128)(2,1)} async-done(((bf16[16,68,768]{2,1,0:T(8,128)(2,1)}), bf16[16,68,768]{2,1,0:T(8,128)(2,1)}, u32[]{:S(2)}, u32[]{:S(2)}) %all-to-all-start.1) | async-done | bytes 1671200 | tf_op jit(solution)/shard_map/all_to_all | solution.py:120
  196.8 13.0 %fusion.115 = bf16[12,64,512]{2,1,0:T(8,128)(2,1)S(1)} fusion(bf16[512,12,64]{0,2,1:T(8,128)(2,1)S(1)} %bitcast.247, f32[12,512]{1,0:T(8,128)S(1)} %fusion.3, f32[12,512]{1,0:T(8,128)S(1)} %get-tuple-element.83, f32[12,512,512]{1,2,0:T(8,128)S(1)} %get-tuple-element.84, pred[512,512]{0,1:T(8,128)(4,1)S(1)} %iota_compare_fusion.23), kind=kOutput, calls=%fused_computation.211 | convolution fusion | flops 418775040 | bytes 14467072 | tf_op jit(solution)/shard_map/hqk,khd->qhd/dot_general | solution.py:60
  216.8 50.0 %all_to_all.41 = bf16[16,68,768]{2,1,0:T(8,128)(2,1)} all-to-all(bf16[16,68,768]{2,1,0:T(8,128)(2,1)} %reshape.386), channel_id=1, replica_groups=mesh['section'=2,'expert'=16] {'expert'}, dimensions={0} | all-to-all | bytes 3342336 | tf_op jit(solution)/shard_map/all_to_all | solution.py:120
  282.9 11.3 %fusion.24 = bf16[1088,768]{1,0:T(8,128)(2,1)} fusion(bf16[2,1,3072,768]{3,2,1,0:T(8,128)(2,1)} %all-gather.11.cloned.1.call-done, f32[1088,3072]{1,0:T(8,128)S(1)} %fusion.22), kind=kOutput, calls=%fused_computation.62 | convolution fusion | flops 5164744704 | bytes 19759104 | tf_op jit(solution)/shard_map/dot_general | solution.py:16
  302.7 35.9 %all-to-all-done.3 = bf16[16,68,768]{2,1,0:T(8,128)(2,1)} async-done(((bf16[16,68,768]{2,1,0:T(8,128)(2,1)}), bf16[16,68,768]{2,1,0:T(8,128)(2,1)}, u32[]{:S(2)}, u32[]{:S(2)}) %all-to-all-start.3) | async-done | bytes 1671200 | tf_op jit(solution)/shard_map/all_to_all | solution.py:120
  354.5 50.5 %all_to_all.42 = bf16[16,68,768]{2,1,0:T(8,128)(2,1)} all-to-all(bf16[16,68,768]{2,1,0:T(8,128)(2,1)} %reshape.390), channel_id=1, replica_groups=mesh['section'=2,'expert'=16] {'expert'}, dimensions={0} | all-to-all | bytes 3342336 | tf_op jit(solution)/shard_map/all_to_all | solution.py:120
  408.4 15.2 %fusion = bf16[1088,3072]{1,0:T(8,128)(2,1)S(1)} fusion(bf16[1088,768]{1,0:T(8,128)(2,1)} %reshape.391, f32[1088,3072]{1,0:T(8,128)} %copy-done.130, bf16[2,1,3072,768]{3,2,1,0:T(8,128)(2,1)} %all-gather.11.cloned.1.call-done), kind=kOutput, calls=%fused_computation.22 | convolution fusion | flops 5200674816 | bytes 26443776 | tf_op jit(solution)/shard_map/dot_general | solution.py:16
  444.6 35.1 %all-to-all-done.5 = bf16[16,68,768]{2,1,0:T(8,128)(2,1)} async-done(((bf16[16,68,768]{2,1,0:T(8,128)(2,1)}), bf16[16,68,768]{2,1,0:T(8,128)(2,1)}, u32[]{:S(2)}, u32[]{:S(2)}) %all-to-all-start.5) | async-done | bytes 1671200 | tf_op jit(solution)/shard_map/all_to_all | solution.py:120
  500.1 9.5 multiply_reduce_fusion.1
  544.5 13.1 %convolution_convert_fusion = bf16[3072,768]{1,0:T(8,128)(2,1)} fusion(bf16[1088,768]{1,0:T(8,128)(2,1)} %reshape.391, f32[1088,3072]{1,0:T(8,128)} %copy-done.130), kind=kOutput, calls=%fused_computation.37 | convolution fusion | flops 5166268416 | bytes 19759104 | tf_op jit(solution)/shard_map/dot_general | solution.py:16
  569.4 12.0 %all-to-all-done.6 = bf16[16,68,768]{2,1,0:T(8,128)(2,1)} async-done(((bf16[16,68,768]{2,1,0:T(8,128)(2,1)}), bf16[16,68,768]{2,1,0:T(8,128)(2,1)}, u32[]{:S(2)}, u32[]{:S(2)}) %all-to-all-start.6) | async-done | bytes 1671200 | tf_op jit(solution)/shard_map/all_to_all | solution.py:120
  583.7 15.3 %fusion.1 = bf16[1088,3072]{1,0:T(8,128)(2,1)S(1)} fusion(bf16[1088,768]{1,0:T(8,128)(2,1)S(1)} %reshape.399, f32[1088,3072]{1,0:T(8,128)} %fusion.19, bf16[2,1,3072,768]{3,2,1,0:T(8,128)(2,1)} %all-gather.11.cloned.1.call-done), kind=kOutput, calls=%fused_computation.23 | convolution fusion | flops 5200674816 | bytes 26443776 | tf_op jit(solution)/shard_map/dot_general | solution.py:16
  622.5 10.5 %convolution_convert_fusion.2 = bf16[768,3072]{1,0:T(8,128)(2,1)} fusion(bf16[1088,768]{1,0:T(8,128)(2,1)} %reshape.387, bf16[1088,3072]{1,0:T(8,128)(2,1)} %copy-done.128), kind=kOutput, calls=%fused_computation.39 | convolution fusion | flops 5136187392 | bytes 13074432 | tf_op jit(solution)/shard_map/dot_general | solution.py:16
  646.9 10.6 %convolution_convert_fusion.3 = bf16[768,3072]{1,0:T(8,128)(2,1)} fusion(bf16[1088,768]{1,0:T(8,128)(2,1)} %reshape.379, bf16[1088,3072]{1,0:T(8,128)(2,1)} %copy-done.129), kind=kOutput, calls=%fused_computation.40 | convolution fusion | flops 5136187392 | bytes 13074432 | tf_op jit(solution)/shard_map/dot_general | solution.py:16
  676.6 9.6 multiply_reduce_fusion
  717.6 68.9 %all-reduce.5.cloned.1.call-done = bf16[1552,768]{1,0:T(8,128)(2,1)} async-done(((bf16[1552,768]{1,0:T(8,128)(2,1)}), bf16[1552,768]{1,0:T(8,128)(2,1)}) %all-reduce.5.cloned.1.call-update) | async-done | bytes 2383888 | tf_op jit(solution)/shard_map/psum | solution.py:219
  788.5 12.8 %convolution_convert_fusion.1 = bf16[3072,768]{1,0:T(8,128)(2,1)} fusion(bf16[1088,768]{1,0:T(8,128)(2,1)S(1)} %copy-done.28, f32[1088,3072]{1,0:T(8,128)} %fusion.19), kind=kOutput, calls=%fused_computation.38 | convolution fusion | flops 5166268416 | bytes 19759104 | tf_op jit(solution)/shard_map/dot_general | solution.py:16
  825.9 115.7 %all-reduce.7.cloned.1.call-done = bf16[1552,768]{1,0:T(8,128)(2,1)} async-done(((bf16[1552,768]{1,0:T(8,128)(2,1)}), bf16[1552,768]{1,0:T(8,128)(2,1)}) %all-reduce.7.cloned.1.call-update) | async-done | bytes 2383888 | tf_op jit(solution)/shard_map/psum | solution.py:219
  943.1 12.9 %fusion.14 = bf16[1,1,768,3072]{3,2,1,0:T(8,128)(2,1)} fusion(bf16[768,3072]{1,0:T(8,128)(2,1)} %collective-permute-done.8, bf16[768,3072]{1,0:T(8,128)(2,1)} %convolution_convert_fusion.2, bf16[768,3072]{1,0:T(8,128)(2,1)} %collective-permute-done.7, bf16[768,3072]{1,0:T(8,128)(2,1)} %convolution_convert_fusion.3, pred[]{:T(512)S(6)} %eq.115), kind=kLoop, calls=%fused_computation.44 | loop fusion | flops 18874368 | bytes 23592960 | tf_op jit(solution)/shard_map/broadcast_in_dim | solution.py:319
  956.1 10.9 %fusion.15 = bf16[1,1,3072,768]{3,2,1,0:T(8,128)(2,1)} fusion(bf16[3072,768]{1,0:T(8,128)(2,1)} %collective-permute-done.10, bf16[3072,768]{1,0:T(8,128)(2,1)} %convolution_convert_fusion, bf16[3072,768]{1,0:T(8,128)(2,1)} %collective-permute-done.9, bf16[3072,768]{1,0:T(8,128)(2,1)} %convolution_convert_fusion.1, pred[]{:T(512)S(6)} %eq.115), kind=kLoop, calls=%fused_computation.45 | loop fusion | flops 18874368 | bytes 23592960 | tf_op jit(solution)/shard_map/broadcast_in_dim | solution.py:320
  (464 shorter events, 333.7 us)
Async XLA Ops:
  7.2 23.0 %all-gather.5.cloned.1.call-start = ((), (), s32[]{:S(2)}) async-start(), calls=%async_computation.8 | async-start | bytes 10616832 | tf_op jit(solution)/shard_map/all_gather | solution.py:238
  7.9 38.7 %all-gather.7.cloned.1.call-start = ((), (), s32[]{:S(2)}) async-start(), calls=%async_computation.9 | async-start | bytes 3538944 | tf_op jit(solution)/shard_map/all_gather | solution.py:238
  8.7 100.2 %all-gather.9.cloned.1.call-start = ((), (), s32[]{:S(2)}) async-start(), calls=%async_computation.10 | async-start | bytes 14155776 | tf_op jit(solution)/shard_map/all_gather | solution.py:238
  9.5 110.3 %all-gather.11.cloned.1.call-start = ((), (), s32[]{:S(2)}) async-start(), calls=%async_computation.11 | async-start | bytes 14155776 | tf_op jit(solution)/shard_map/all_gather | solution.py:238
  11.1 132.9 %copy-start.61 = (s32[512,1]{0,1:T(1,128)}, s32[512,1]{0,1:T(1,128)S(1)}, u32[]{:S(2)}) copy-start(s32[512,1]{0,1:T(1,128)S(1)} %get-tuple-element.105) | copy-start | bytes 6148
  11.1 132.9 %copy-start.63 = (s32[512,1]{0,1:T(1,128)}, s32[512,1]{0,1:T(1,128)S(1)}, u32[]{:S(2)}) copy-start(s32[512,1]{0,1:T(1,128)S(1)} %get-tuple-element.106) | copy-start | bytes 6148
  136.2 41.2 %all-to-all-start.1 = ((bf16[16,68,768]{2,1,0:T(8,128)(2,1)}), bf16[16,68,768]{2,1,0:T(8,128)(2,1)}, u32[]{:S(2)}, u32[]{:S(2)}) async-start(bf16[16,68,768]{2,1,0:T(8,128)(2,1)} %reshape.380), calls=%async_computation.1 | async-start | bytes 3538944 | tf_op jit(solution)/shard_map/all_to_all | solution.py:120
  297.6 41.0 %all-to-all-start.3 = ((bf16[16,68,768]{2,1,0:T(8,128)(2,1)}), bf16[16,68,768]{2,1,0:T(8,128)(2,1)}, u32[]{:S(2)}, u32[]{:S(2)}) async-start(bf16[16,68,768]{2,1,0:T(8,128)(2,1)} %reshape.388), calls=%async_computation.3 | async-start | bytes 3538944 | tf_op jit(solution)/shard_map/all_to_all | solution.py:120
  438.7 41.0 %all-to-all-start.5 = ((bf16[16,68,768]{2,1,0:T(8,128)(2,1)}), bf16[16,68,768]{2,1,0:T(8,128)(2,1)}, u32[]{:S(2)}, u32[]{:S(2)}) async-start(bf16[16,68,768]{2,1,0:T(8,128)(2,1)} %reshape.392), calls=%async_computation.5 | async-start | bytes 3538944 | tf_op jit(solution)/shard_map/all_to_all | solution.py:120
  535.8 45.6 %all-to-all-start.6 = ((bf16[16,68,768]{2,1,0:T(8,128)(2,1)}), bf16[16,68,768]{2,1,0:T(8,128)(2,1)}, u32[]{:S(2)}, u32[]{:S(2)}) async-start(bf16[16,68,768]{2,1,0:T(8,128)(2,1)} %reshape.398), calls=%async_computation.6 | async-start | bytes 3538944 | tf_op jit(solution)/shard_map/all_to_all | solution.py:120
  569.4 73.1 %collective-permute-start.3 = (bf16[1552,768]{1,0:T(8,128)(2,1)}, bf16[1552,768]{1,0:T(8,128)(2,1)}, u32[]{:S(2)}, u32[]{:S(2)}) collective-permute-start(bf16[1552,768]{1,0:T(8,128)(2,1)} %constant_dynamic-slice_fusion.1), channel_id=1, source_target_pairs={{0,16},{16,0},{1,17},{17,1},{2,18},{18,2},{3,19},{19,3},{4,20},{20... | collective-permute-start | bytes 7151624 | tf_op jit(solution)/shard_map/ppermute | solution.py:218
  614.2 46.3 %all-to-all-start.7 = ((bf16[16,68,768]{2,1,0:T(8,128)(2,1)}), bf16[16,68,768]{2,1,0:T(8,128)(2,1)S(1)}, u32[]{:S(2)}, u32[]{:S(2)}) async-start(bf16[16,68,768]{2,1,0:T(8,128)(2,1)} %reshape.400), calls=%async_computation.7 | async-start | bytes 3538944 | tf_op jit(solution)/shard_map/all_to_all | solution.py:120
  622.4 164.1 %all-reduce.5.cloned.1.call-start = ((), (), s32[]{:S(2)}) async-start(), calls=%async_computation.12 | async-start | bytes 4767744 | tf_op jit(solution)/shard_map/psum | solution.py:219
  632.9 193.0 %collective-permute-start.8 = (bf16[768,3072]{1,0:T(8,128)(2,1)}, bf16[768,3072]{1,0:T(8,128)(2,1)}, u32[]{:S(2)}, u32[]{:S(2)}) collective-permute-start(bf16[768,3072]{1,0:T(8,128)(2,1)} %convolution_convert_fusion.2), channel_id=1, source_target_pairs={{0,16},{1,17},{2,18},{3,19},{4,20},{5,21},{6,22},{7,23},{8,24},{9,... | collective-permute-start | bytes 14155784 | tf_op jit(solution)/shard_map/ppermute | solution.py:269
  636.4 319.6 %collective-permute-start.10 = (bf16[3072,768]{1,0:T(8,128)(2,1)}, bf16[3072,768]{1,0:T(8,128)(2,1)}, u32[]{:S(2)}, u32[]{:S(2)}) collective-permute-start(bf16[3072,768]{1,0:T(8,128)(2,1)} %convolution_convert_fusion), channel_id=1, source_target_pairs={{0,16},{1,17},{2,18},{3,19},{4,20},{5,21},{6,22},{7,23},{8,24},{9,... | collective-permute-start | bytes 14155784 | tf_op jit(solution)/shard_map/ppermute | solution.py:270
  639.8 161.4 %collective-permute-start.1 = (bf16[512,768]{1,0:T(8,128)(2,1)}, bf16[512,768]{1,0:T(8,128)(2,1)}, u32[]{:S(2)}, u32[]{:S(2)}) collective-permute-start(bf16[512,768]{1,0:T(8,128)(2,1)} %get-tuple-element.45), channel_id=1, source_target_pairs={{0,16},{1,17},{2,18},{3,19},{4,20},{5,21},{6,22},{7,23},{8,24},{9,... | collective-permute-start | bytes 2359304 | tf_op jit(solution)/shard_map/ppermute | solution.py:271
  646.9 294.8 %all-reduce.7.cloned.1.call-start = ((), (), s32[]{:S(2)}) async-start(), calls=%async_computation.13 | async-start | bytes 4767744 | tf_op jit(solution)/shard_map/psum | solution.py:219
  657.5 285.6 %collective-permute-start.7 = (bf16[768,3072]{1,0:T(8,128)(2,1)}, bf16[768,3072]{1,0:T(8,128)(2,1)}, u32[]{:S(2)}, u32[]{:S(2)}) collective-permute-start(bf16[768,3072]{1,0:T(8,128)(2,1)} %convolution_convert_fusion.3), channel_id=1, source_target_pairs={{16,0},{17,1},{18,2},{19,3},{20,4},{21,5},{22,6},{23,7},{24,8},{25... | collective-permute-start | bytes 14155784 | tf_op jit(solution)/shard_map/ppermute | solution.py:276
  788.3 14.2 %collective-permute-start.4 = (bf16[1552,768]{1,0:T(8,128)(2,1)S(1)}, bf16[1552,768]{1,0:T(8,128)(2,1)S(1)}, u32[]{:S(2)}, u32[]{:S(2)}) collective-permute-start(bf16[1552,768]{1,0:T(8,128)(2,1)S(1)} %constant_dynamic-slice_fusion), channel_id=1, source_target_pairs={{0,16},{16,0},{1,17},{17,1},{2,18},{18,2},{3,19},{19,3},{4,20},{20... | collective-permute-start | bytes 7151624 | tf_op jit(solution)/shard_map/ppermute | solution.py:218
  801.3 154.8 %collective-permute-start.9 = (bf16[3072,768]{1,0:T(8,128)(2,1)}, bf16[3072,768]{1,0:T(8,128)(2,1)}, u32[]{:S(2)}, u32[]{:S(2)}) collective-permute-start(bf16[3072,768]{1,0:T(8,128)(2,1)} %convolution_convert_fusion.1), channel_id=1, source_target_pairs={{16,0},{17,1},{18,2},{19,3},{20,4},{21,5},{22,6},{23,7},{24,8},{25... | collective-permute-start | bytes 14155784 | tf_op jit(solution)/shard_map/ppermute | solution.py:277
  802.6 10.6 %collective-permute-start = (bf16[512,768]{1,0:T(8,128)(2,1)}, bf16[512,768]{1,0:T(8,128)(2,1)}, u32[]{:S(2)}, u32[]{:S(2)}) collective-permute-start(bf16[512,768]{1,0:T(8,128)(2,1)} %get-tuple-element.65), channel_id=1, source_target_pairs={{0,16},{16,0},{1,17},{17,1},{2,18},{18,2},{3,19},{19,3},{4,20},{20... | collective-permute-start | bytes 2359304 | tf_op jit(solution)/shard_map/ppermute | solution.py:263
  813.1 5.3 collective-permute-start.2
  818.4 148.6 %collective-permute-start.5 = (bf16[1552,768]{1,0:T(8,128)(2,1)S(1)}, bf16[1552,768]{1,0:T(8,128)(2,1)}, u32[]{:S(2)}, u32[]{:S(2)}) collective-permute-start(bf16[1552,768]{1,0:T(8,128)(2,1)S(1)} %copy-done.26), channel_id=1, source_target_pairs={{0,16},{1,17},{2,18},{3,19},{4,20},{5,21},{6,22},{7,23},{8,24},{9,... | collective-permute-start | bytes 7151624 | tf_op jit(solution)/shard_map/ppermute | solution.py:273
  941.6 27.3 %collective-permute-start.6 = (bf16[1552,768]{1,0:T(8,128)(2,1)}, bf16[1552,768]{1,0:T(8,128)(2,1)}, u32[]{:S(2)}, u32[]{:S(2)}) collective-permute-start(bf16[1552,768]{1,0:T(8,128)(2,1)} %all-reduce.7.cloned.1.call-done), channel_id=1, source_target_pairs={{16,0},{17,1},{18,2},{19,3},{20,4},{21,5},{22,6},{23,7},{24,8},{25... | collective-permute-start | bytes 7151624 | tf_op jit(solution)/shard_map/ppermute | solution.py:281
  (137 other events, 1441.4 us)
Sparse Core Ops, SparseCore 0:
  9.6 20.6 all-gather.4
  31.7 12.1 all-gather.6
  45.5 23.0 all-gather.8
  69.9 23.0 all-gather.10
  647.0 139.4 all-reduce.4
  809.8 131.7 all-reduce.6
